TPU v7x, 32 devices: a whole 2x2x4 slice. The times are simulated.
32 devices in a mesh: groups: 2 (over y), blk: 4 (over z), side: 2 (over x), tp: 2 (over core).
Axes of the slice: x: 2, y: 2, z: 4, core: 2. Of those that a mesh axis runs over, the one named last changes fastest.
Arguments:
- queries: bfloat16 [4, 512, 4096], P(('groups', 'side'), 'blk', 'tp'), parts along dimension 0, may hold values from -8 to 8
- key_rows: bfloat16 [4, 512, 256], P(('groups', 'side'), 'blk', 'tp'), parts along dimension 0, may hold values from -8 to 8
- value_rows: bfloat16 [4, 512, 256], P(('groups', 'side'), 'blk', 'tp'), parts along dimension 0, may hold values from -6 to 6
- segments: int32 [4, 512], P(('groups', 'side'), 'blk'), parts along dimension 0, may hold values from 0 to 1, never falling along the last dimension, each value on 1 to 384 neighbouring positions
- hidden_entry_rows: bfloat16 [4, 512, 4096], P(('groups', 'side'), 'blk', 'tp'), parts along dimension 0, may hold values from -6 to 6
- expert_ids: int32 [4, 512, 8], P(('groups', 'side'), 'blk'), parts along dimension 0, may hold values from 0 to 127, all different within a row; in each aligned block of 128 rows (0 to 127, 128 to 255, ..., all dimensions but the last counted through in order) at most 10 rows name the same one
- route_weight: float32 [4, 512, 8], P(('groups', 'side'), 'blk'), parts along dimension 0, may hold values from 0.2 to 1
- w_gate: bfloat16 [4, 2048, 1536], P('blk', 'tp', 'side'), may hold values from -0.09375 to 0.09375
- w_up: bfloat16 [4, 2048, 1536], P('blk', 'tp', 'side'), may hold values from -0.09375 to 0.09375
- w_down: bfloat16 [4, 1536, 2048], P('blk', 'side', 'tp'), may hold values from -0.15625 to 0.15625
Outputs:
- attended: bfloat16 [4, 512, 4096], P(('groups', 'side'), 'blk', 'tp'), parts along dimension 0
- moe_out: bfloat16 [4, 512, 4096], P(('groups', 'side'), 'blk', 'tp'), parts along dimension 0
There are 2 independent parts, one for each index of `groups`. A program takes and returns all parts, laid end to end along the dimension named above; an argument that names none is the same for every part. Nothing has to cross between parts.
Inputs may be any that keep to these rules, and one draw needn't show every extreme that they name: `expert_ids`: in the 128 rows of one device (aligned blocks of rows of a sequence) no expert is named by more than 10 rows, and in some such block one is named by exactly 10; a row names 8 different experts. `segments`: document numbers never fall along a sequence; a document spans at most 384 positions, and one spans exactly that many.
All inputs are finite; a program needn't handle non-finite values.
Results may differ from a plain program's by a relative error of at most 0.02.
Values may be sent and summed in bfloat16 or wider, within the bound.
A program may use at most 64 MiB of HBM per device.

v0:
```python
import math
import jax
import jax.numpy as jnp
from jax import lax
from jax.sharding import PartitionSpec as P

HEAD_DIM = 128
CAP = 10


def passed_along(value, axis, steps):
    count = lax.axis_size(axis)
    pairs = [(source, (source + steps) % count) for source in range(count)]
    return lax.ppermute(value, axis, pairs)


def slot_choice(id_rows, experts, capacity):
    named = id_rows[:, :, None] == jnp.arange(experts, dtype=jnp.int32)[None, None, :]
    hits = jnp.sum(named.astype(jnp.int32), axis=1)
    ranks = jnp.cumsum(hits, axis=0) - hits
    levels = jnp.arange(capacity, dtype=jnp.int32)[None, :, None]
    return (hits.T[:, None, :] > 0) & (ranks.T[:, None, :] == levels)


def routing_slot_index(id_rows, experts, capacity):
    chosen = slot_choice(id_rows, experts, capacity)
    row_iota = jnp.arange(id_rows.shape[0], dtype=jnp.int32)
    index = jnp.sum(jnp.where(chosen, row_iota[None, None, :], 0), axis=2)
    valid = jnp.any(chosen, axis=2)
    return (index, valid)


def pick_rows(rows, index, valid):
    taken = jnp.take(rows, index, axis=0)
    return jnp.where(valid[..., None], taken, jnp.zeros((), rows.dtype))


def slot_weights(id_rows, weight_rows, experts, capacity):
    named = id_rows[:, :, None] == jnp.arange(experts, dtype=jnp.int32)[None, None, :]
    shares = jnp.sum(jnp.where(named, weight_rows[:, :, None], 0.0), axis=1)
    chosen = slot_choice(id_rows, experts, capacity)
    return chosen.astype(jnp.float32) * shares.T[:, None, :]


def body(
    queries,
    key_rows,
    value_rows,
    segments,
    hidden_entry_rows,
    expert_ids,
    route_weight,
    w_gate,
    w_up,
    w_down,
):
    length = queries.shape[1]
    head_size = HEAD_DIM
    kv_here = key_rows.shape[2] // head_size
    group = queries.shape[2] // (head_size * kv_here)
    query_portion = queries[0].reshape(length, kv_here, group, head_size)
    local_segment_labels = segments[0]
    query_pos = lax.axis_index("blk") * length + jnp.arange(length, dtype=jnp.int32)
    factor = 1.0 / math.sqrt(head_size)
    start_state = (
        jnp.full((length, kv_here, group), -1e30, jnp.float32),
        jnp.zeros((length, kv_here, group), jnp.float32),
        jnp.zeros((length, kv_here, group, head_size), jnp.float32),
    )
    key_piece = lax.all_gather(key_rows[0], "blk", axis=0, tiled=True)
    value_fragment = lax.all_gather(value_rows[0], "blk", axis=0, tiled=True)
    segment_piece = lax.all_gather(local_segment_labels, "blk", axis=0, tiled=True)
    rows_in = key_piece.shape[0]
    width = math.gcd(rows_in, 512)

    def one_block(block_index, state):
        row_max, totals, accumulated = state
        begin = block_index * width
        key_tile_block = lax.dynamic_slice_in_dim(key_piece, begin, width, 0).reshape(
            width, kv_here, head_size
        )
        value_block = lax.dynamic_slice_in_dim(value_fragment, begin, width, 0).reshape(
            width, kv_here, head_size
        )
        segment_block = lax.dynamic_slice_in_dim(segment_piece, begin, width, 0)
        key_pos = begin + jnp.arange(width, dtype=jnp.int32)
        allowed = (key_pos[None, :] <= query_pos[:, None]) & (
            segment_block[None, :] == local_segment_labels[:, None]
        )
        masking = allowed[:, None, None, :]
        scores = (
            jnp.einsum(
                "wsmz,usz->wsmu", query_portion, key_tile_block, preferred_element_type=jnp.float32
            )
            * factor
        )
        scores = jnp.where(masking, scores, -1e30)
        new_max = jnp.maximum(row_max, jnp.max(scores, axis=3))
        rescale = jnp.exp(row_max - new_max)
        weights = jnp.where(masking, jnp.exp(scores - new_max[..., None]), 0.0)
        totals = totals * rescale + jnp.sum(weights, axis=3)
        update = jnp.einsum(
            "jzre,ezm->jzrm",
            weights.astype(jnp.bfloat16),
            value_block,
            preferred_element_type=jnp.float32,
        )
        accumulated = accumulated * rescale[..., None] + update
        return (new_max, totals, accumulated)

    row_max, totals, accumulated = lax.fori_loop(0, rows_in // width, one_block, start_state)
    attended = (
        (accumulated / totals[..., None])
        .astype(jnp.bfloat16)
        .reshape(1, length, group * kv_here * head_size)
    )
    experts = lax.axis_size("blk") // 2
    capacity = CAP
    ff_here = w_gate.shape[2]
    quarter = hidden_entry_rows.shape[2] // 2
    index, valid = routing_slot_index(expert_ids[0], experts, capacity)
    taken = pick_rows(hidden_entry_rows[0], index, valid)
    outgoing = (
        taken.reshape(experts, capacity, 2, quarter)
        .transpose(2, 0, 1, 3)
        .reshape(2 * experts, capacity, quarter)[:, None]
    )
    arrived = lax.all_to_all(outgoing, "blk", split_axis=0, concat_axis=0, tiled=True)
    shards = lax.all_gather(arrived, "side", axis=1, tiled=True)
    gate_piece = jnp.einsum("bscd,df->bscf", shards, w_gate[0], preferred_element_type=jnp.float32)
    up_piece = jnp.einsum("bscd,df->bscf", shards, w_up[0], preferred_element_type=jnp.float32)
    projected = jnp.concatenate([gate_piece, up_piece], axis=3)
    gate_part = projected[..., :ff_here]
    up_part = projected[..., ff_here:]
    gate_sum, up_sum = (
        lax.psum(gate_part.astype(jnp.bfloat16), "tp").astype(jnp.float32),
        lax.psum(up_part.astype(jnp.bfloat16), "tp").astype(jnp.float32),
    )
    both_sums = jnp.stack([gate_sum, up_sum])
    partner_sums = passed_along(
        both_sums.astype(jnp.bfloat16), "blk", lax.axis_size("blk") // 2
    ).astype(both_sums.dtype)
    full_sums = both_sums + partner_sums
    hidden = (jax.nn.silu(full_sums[0]) * full_sums[1]).astype(jnp.bfloat16)
    part_out = jnp.einsum(
        "bscf,fd->bscd", hidden, w_down[0], preferred_element_type=jnp.float32
    ).astype(jnp.bfloat16)
    parts = lax.all_to_all(part_out, "side", split_axis=1, concat_axis=1, tiled=True)
    slot_out = jnp.sum(parts, axis=1, dtype=jnp.float32).astype(jnp.bfloat16)
    returned = lax.all_to_all(slot_out, "blk", split_axis=0, concat_axis=0, tiled=True)
    returned_split = returned.astype(jnp.float32).reshape(2, experts, capacity, quarter)
    own_weighted = slot_weights(expert_ids[0], route_weight[0], experts, capacity)
    mixed = jnp.einsum(
        "ecr,kecq->rkq", own_weighted, returned_split, precision=lax.Precision.HIGHEST
    )
    moe_out = mixed.reshape(mixed.shape[0], 2 * quarter).astype(jnp.bfloat16)[None]
    return (attended, moe_out)


def solution(mesh):
    placed = (
        P(("groups", "side"), "blk", "tp"),
        P(("groups", "side"), "blk", "tp"),
        P(("groups", "side"), "blk", "tp"),
        P(("groups", "side"), "blk"),
        P(("groups", "side"), "blk", "tp"),
        P(("groups", "side"), "blk", None),
        P(("groups", "side"), "blk", None),
        P("blk", "tp", "side"),
        P("blk", "tp", "side"),
        P("blk", "side", "tp"),
    )
    return jax.shard_map(
        body,
        mesh=mesh,
        in_specs=placed,
        out_specs=(P(("groups", "side"), "blk", "tp"), P(("groups", "side"), "blk", "tp")),
        check_vma=False,
    )
```

profile of v0, /device:TPU:0, one launch (start us, length us, event | category | flops | bytes accessed | tf_op | source)
XLA Modules:
  0.0 131.0 jit_solution(2119913399250369770)
XLA Ops:
  7.2 0.8 convert_reduce_fusion
  8.0 0.1 copy.47
  8.1 0.2 reduce_window_sum.12
  8.4 0.1 select_reduce_fusion
  8.5 0.1 fusion.50
  8.7 1.8 %gather_fusion = bf16[20,2048]{1,0:T(8,128)(2,1)S(1)} fusion(bf16[128,2048]{1,0:T(8,128)(2,1)} %bitcast.124, s32[1024]{0:T(1024)S(1)} %pad_clamp_fusion), kind=kCustom, calls=%fused_computation | custom fusion | bytes 163920 | tf_op jit(solution)/shard_map/jit(_take)/gather | solution.py:34
  10.6 0.7 fusion.47
  11.3 6.3 %all-to-all-start = ((bf16[4,1,10,1024]{3,2,1,0:T(8,128)(2,1)}), bf16[4,1,10,1024]{3,2,1,0:T(8,128)(2,1)S(1)}, u32[]{:S(2)}, u32[]{:S(2)}) async-start(bf16[4,1,10,1024]{3,2,1,0:T(8,128)(2,1)} %bitcast.21), calls=%async_computation | async-start | bytes 262144 | tf_op jit(solution)/shard_map/all_to_all | solution.py:128
  17.7 11.5 %all-gather = s32[1,512]{1,0:T(1,128)S(1)} all-gather(s32[1,128]{1,0:T(1,128)} %param.13), channel_id=2, replica_groups=mesh['groups'=2,'blk'=4,'side'=2,'tp'=2] {'blk'}, dimensions={1}, use_global_device_ids=true | all-gather | bytes 2560 | tf_op jit(solution)/shard_map/all_gather | solution.py:72
  29.2 0.8 fusion.41
  30.0 1.1 copy.62
  31.2 13.6 %all-gather.1 = bf16[1,512,128]{2,1,0:T(8,128)(2,1)S(1)} all-gather(bf16[1,128,128]{2,1,0:T(8,128)(2,1)} %param.11), channel_id=3, replica_groups=mesh['groups'=2,'blk'=4,'side'=2,'tp'=2] {'blk'}, dimensions={1}, use_global_device_ids=true | all-gather | bytes 163840 | tf_op jit(solution)/shard_map/all_gather | solution.py:70
  44.8 5.6 %all_gather.15 = bf16[4,2,10,1024]{3,2,1,0:T(8,128)(2,1)S(1)} all-gather(bf16[4,1,10,1024]{3,2,1,0:T(8,128)(2,1)S(1)} %all-to-all-done), channel_id=1, replica_groups=mesh['groups'=2,'blk'=4,'side'=2,'tp'=2] {'side'}, dimensions={1}, use_global_device_ids=true | all-gather | bytes 245760 | tf_op jit(solution)/shard_map/all_gather | solution.py:129
  50.4 2.5 %fusion.33 = bf16[1,4,2,10,768]{4,3,2,1,0:T(8,128)(2,1)} fusion(bf16[4,2,10,1024]{3,2,1,0:T(8,128)(2,1)S(1)} %all_gather.15, bf16[1,1024,768]{2,1,0:T(8,128)(2,1)} %param.17), kind=kOutput, calls=%fused_computation.24 | convolution fusion | flops 125890560 | bytes 1859584 | tf_op jit(solution)/shard_map/bscd,df->bscf/dot_general | solution.py:130
  52.8 2.5 %fusion.30 = bf16[1,4,2,10,768]{4,3,2,1,0:T(8,128)(2,1)} fusion(bf16[4,2,10,1024]{3,2,1,0:T(8,128)(2,1)S(1)} %all_gather.15, bf16[1,1024,768]{2,1,0:T(8,128)(2,1)} %param.18), kind=kOutput, calls=%fused_computation.23 | convolution fusion | flops 125890560 | bytes 1859584 | tf_op jit(solution)/shard_map/bscd,df->bscf/dot_general | solution.py:131
  55.3 2.7 %fusion = (f32[128,16]{0,1:T(8,128)S(1)}, f32[512,128,16]{1,0,2:T(8,128)}) fusion(pred[128,512]{0,1:T(8,128)(4,1)S(1)} %fusion.41, bf16[128,16,128]{2,1,0:T(8,128)(2,1)S(1)} %bitcast.123, bf16[1,512,128]{2,1,0:T(8,128)(2,1)S(1)} %all-gather.1), kind=kOutput, calls=%fused_computation.3 | convolution fusion | flops 271579136 | bytes 4923392 | tf_op jit(solution)/shard_map/while/body/eval_jaxpr/wsmz,usz->wsmu/dot_general | solution.py:92
  58.0 14.2 %all-reduce.3.cloned.1.call-done = (bf16[1,4,2,10,768]{4,3,2,1,0:T(8,128)(2,1)}, bf16[1,4,2,10,768]{4,3,2,1,0:T(8,128)(2,1)}) async-done(((bf16[1,4,2,10,768]{4,3,2,1,0:T(8,128)(2,1)}, bf16[1,4,2,10,768]{4,3,2,1,0:T(8,128)(2,1)}), (bf16[1,4,2,10,768]{4,3,2,1,0:T(8,128)(2,1)}, bf16[1,4,2,10,768]{4,3,2,1,0:T(8,128)(2,1)})) %all-reduce.3.cloned.1.call-update) | async-done | bytes 245776 | tf_op jit(solution)/shard_map/psum | solution.py:136
  72.2 0.9 constant_dynamic-update-slice_fusion.1
  73.2 0.9 constant_dynamic-update-slice_fusion
  74.1 2.8 %collective-permute-start = (bf16[2,4,2,10,768]{4,3,2,1,0:T(8,128)(2,1)S(1)}, bf16[2,4,2,10,768]{4,3,2,1,0:T(8,128)(2,1)S(1)}, u32[]{:S(2)}, u32[]{:S(2)}) collective-permute-start(bf16[2,4,2,10,768]{4,3,2,1,0:T(8,128)(2,1)S(1)} %constant_dynamic-update-slice_fusion), channel_id=1, source_target_pairs={{0,8},{4,12},{8,0},{12,4},{1,9},{5,13},{9,1},{13,5},{2,10},{6,14},... | collective-permute-start | bytes 737288 | tf_op jit(solution)/shard_map/ppermute | solution.py:14
  76.9 3.2 %fusion.1 = f32[128,16]{0,1:T(8,128)S(1)} fusion(f32[512,128,16]{1,0,2:T(8,128)} %get-tuple-element.48, f32[128,16]{0,1:T(8,128)S(1)} %broadcast_maximum_fusion, pred[128,512]{0,1:T(8,128)(4,1)S(1)} %fusion.41), kind=kLoop, calls=%fused_computation.4 | loop fusion | flops 5240832 | bytes 4276224 | tf_op jit(solution)/shard_map/while/body/eval_jaxpr/reduce_sum | solution.py:101
  80.1 14.7 %collective-permute-done = bf16[2,4,2,10,768]{4,3,2,1,0:T(8,128)(2,1)S(1)} collective-permute-done((bf16[2,4,2,10,768]{4,3,2,1,0:T(8,128)(2,1)S(1)}, bf16[2,4,2,10,768]{4,3,2,1,0:T(8,128)(2,1)S(1)}, u32[]{:S(2)}, u32[]{:S(2)}) %collective-permute-start) | collective-permute-done | bytes 245792 | tf_op jit(solution)/shard_map/ppermute | solution.py:14
  95.0 0.4 fusion.21
  95.4 0.8 copy.51
  96.2 3.4 %all-to-all-start.1 = ((bf16[4,2,10,1024]{3,0,2,1:T(4,128)(2,1)}), bf16[4,2,10,1024]{3,0,2,1:T(4,128)(2,1)S(1)}, u32[]{:S(2)}, u32[]{:S(2)}) async-start(bf16[4,2,10,1024]{3,0,2,1:T(4,128)(2,1)} %copy.51), calls=%async_computation.1 | async-start | bytes 327680 | tf_op jit(solution)/shard_map/all_to_all | solution.py:148
  99.8 12.3 %all-gather.2 = bf16[1,512,128]{1,2,0:T(8,128)(2,1)S(1)} all-gather(bf16[1,128,128]{1,2,0:T(8,128)(2,1)S(1)} %copy.45), channel_id=4, replica_groups=mesh['groups'=2,'blk'=4,'side'=2,'tp'=2] {'blk'}, dimensions={1}, use_global_device_ids=true | all-gather | bytes 163840 | tf_op jit(solution)/shard_map/all_gather | solution.py:71
  112.1 0.7 copy.61
  112.8 3.9 %all-to-all-start.2 = ((bf16[4,10,1024]{2,1,0:T(8,128)(2,1)}), bf16[4,10,1024]{2,1,0:T(8,128)(2,1)S(1)}, u32[]{:S(2)}, u32[]{:S(2)}) async-start(bf16[4,10,1024]{2,1,0:T(8,128)(2,1)} %copy.61), calls=%async_computation.2 | async-start | bytes 262144 | tf_op jit(solution)/shard_map/all_to_all | solution.py:150
  116.7 3.4 %divide_convert_fusion = bf16[1,128,128,16]{2,1,3,0:T(8,128)(2,1)S(1)} fusion(f32[512,128,16]{1,0,2:T(8,128)} %get-tuple-element.48, f32[128,16]{0,1:T(8,128)S(1)} %broadcast_maximum_fusion, pred[128,512]{0,1:T(8,128)(4,1)S(1)} %fusion.41, f32[128,16]{0,1:T(8,128)S(1)} %get-tuple-element.46, f32[128,16]{0,1:T(8,128)S(1)} %get-tuple-element.45, ...), kind=kOutput, calls=%fused_computation.25 | convolution fusion | flops 274464768 | bytes 4939776 | tf_op jit(solution)/shard_map/while/body/eval_jaxpr/jzre,ezm->jzrm/dot_general | solution.py:102
  120.1 1.0 copy.55
  121.1 1.4 %all-to-all-done.2 = bf16[4,10,1024]{2,1,0:T(8,128)(2,1)S(1)} async-done(((bf16[4,10,1024]{2,1,0:T(8,128)(2,1)}), bf16[4,10,1024]{2,1,0:T(8,128)(2,1)S(1)}, u32[]{:S(2)}, u32[]{:S(2)}) %all-to-all-start.2) | async-done | bytes 81952 | tf_op jit(solution)/shard_map/all_to_all | solution.py:150
  122.7 1.4 %fusion.4 = bf16[1,128,2048]{2,1,0:T(8,128)(2,1)} fusion(bf16[2048,10,2]{0,2,1:T(2,128)(2,1)S(1)} %bitcast.125, f32[2,128]{1,0:T(2,128)S(1)} %bitcast.132, s32[2,128]{1,0:T(2,128)S(1)} %copy.49, pred[2,128]{1,0:T(4,128)(4,1)S(1)} %compare_bitcast_fusion), kind=kOutput, calls=%fused_computation.8 | convolution fusion | flops 63184384 | bytes 608512 | tf_op jit(solution)/shard_map/ecr,kecq->rkq/dot_general | solution.py:153
  (28 shorter events, 0.7 us)
Async XLA Ops:
  7.2 87.8 %copy-start = (bf16[1,768,1024]{2,1,0:T(8,128)(2,1)S(1)}, bf16[1,768,1024]{2,1,0:T(8,128)(2,1)}, u32[]{:S(2)}) copy-start(bf16[1,768,1024]{2,1,0:T(8,128)(2,1)} %param.19) | copy-start | bytes 4718596
  11.3 33.4 %all-to-all-start = ((bf16[4,1,10,1024]{3,2,1,0:T(8,128)(2,1)}), bf16[4,1,10,1024]{3,2,1,0:T(8,128)(2,1)S(1)}, u32[]{:S(2)}, u32[]{:S(2)}) async-start(bf16[4,1,10,1024]{3,2,1,0:T(8,128)(2,1)} %bitcast.21), calls=%async_computation | async-start | bytes 262144 | tf_op jit(solution)/shard_map/all_to_all | solution.py:128
  17.7 54.5 %all-reduce.3.cloned.1.call-start = ((), (), s32[]{:S(2)}) async-start(), calls=%async_computation.3 | async-start | bytes 786432 | tf_op jit(solution)/shard_map/psum | solution.py:136
  74.1 20.7 %collective-permute-start = (bf16[2,4,2,10,768]{4,3,2,1,0:T(8,128)(2,1)S(1)}, bf16[2,4,2,10,768]{4,3,2,1,0:T(8,128)(2,1)S(1)}, u32[]{:S(2)}, u32[]{:S(2)}) collective-permute-start(bf16[2,4,2,10,768]{4,3,2,1,0:T(8,128)(2,1)S(1)} %constant_dynamic-update-slice_fusion), channel_id=1, source_target_pairs={{0,8},{4,12},{8,0},{12,4},{1,9},{5,13},{9,1},{13,5},{2,10},{6,14},... | collective-permute-start | bytes 737288 | tf_op jit(solution)/shard_map/ppermute | solution.py:14
  76.9 22.8 %copy-start.1 = (bf16[1,128,128]{2,1,0:T(8,128)(2,1)S(1)}, bf16[1,128,128]{2,1,0:T(8,128)(2,1)}, u32[]{:S(2)}) copy-start(bf16[1,128,128]{2,1,0:T(8,128)(2,1)} %param.12) | copy-start | bytes 98308
  96.2 15.8 %all-to-all-start.1 = ((bf16[4,2,10,1024]{3,0,2,1:T(4,128)(2,1)}), bf16[4,2,10,1024]{3,0,2,1:T(4,128)(2,1)S(1)}, u32[]{:S(2)}, u32[]{:S(2)}) async-start(bf16[4,2,10,1024]{3,0,2,1:T(4,128)(2,1)} %copy.51), calls=%async_computation.1 | async-start | bytes 327680 | tf_op jit(solution)/shard_map/all_to_all | solution.py:148
  112.8 9.8 %all-to-all-start.2 = ((bf16[4,10,1024]{2,1,0:T(8,128)(2,1)}), bf16[4,10,1024]{2,1,0:T(8,128)(2,1)S(1)}, u32[]{:S(2)}, u32[]{:S(2)}) async-start(bf16[4,10,1024]{2,1,0:T(8,128)(2,1)} %copy.61), calls=%async_computation.2 | async-start | bytes 262144 | tf_op jit(solution)/shard_map/all_to_all | solution.py:150
  116.7 4.4 %copy-start.2 = (s32[1,128,8]{1,2,0:T(8,128)S(1)}, s32[1,128,8]{1,2,0:T(8,128)}, u32[]{:S(2)}) copy-start(s32[1,128,8]{1,2,0:T(8,128)} %param.15) | copy-start | bytes 12292
  116.7 4.5 %copy-start.3 = (f32[1,128,8]{1,2,0:T(8,128)S(1)}, f32[1,128,8]{1,2,0:T(8,128)}, u32[]{:S(2)}) copy-start(f32[1,128,8]{1,2,0:T(8,128)} %param.16) | copy-start | bytes 12292
Sparse Core Ops, SparseCore 0:
  55.4 16.7 all-reduce.2
where the time goes:
time: 132 us; the launch traced here: 131 us
  blocking collectives  43 us (33%)
  waiting for transfers between devices  30.4 us (23%)
  starting transfers between devices  16.4 us (12%)
  between operations  14.2 us (11%)
  matrix products  12.9 us (10%)
  local copies, waits for them, and re-layouts  7.85 us (6%)
  other arithmetic  6.27 us (5%)
    ppermute x1, waiting for transfers between devices, passed_along(): return lax.ppermute(value, axis, pairs)  14.7 us
    psum x1, waiting for transfers between devices, body(): lax.psum(gate_part.astype(jnp.bfloat16), 'tp').astype(jnp.float32)  14.2 us
    all_gather x1, blocking collectives, body(): key_piece = lax.all_gather(key_rows[0], 'blk', axis=0, tiled=True)  13.6 us
    all_gather x1, blocking collectives, body(): value_fragment = lax.all_gather(value_rows[0], 'blk', axis=0, tiled=True)  12.3 us
    all_gather x1, blocking collectives, body(): lax.all_gather(local_segment_labels, 'blk', axis=0, tiled=True)  11.5 us
    all_to_all x1, starting transfers between devices, body(): lax.all_to_all(outgoing, 'blk', split_axis=0, concat_axis=0, tiled=True)  6.35 us
    all_gather x1, blocking collectives, body(): shards = lax.all_gather(arrived, 'side', axis=1, tiled=True)  5.63 us
    unnamed x13, local copies, waits for them, and re-layouts  3.93 us
  transfers between devices with their start and end apart: 5, of which 3 were waited for; matrix products, arithmetic and copies ran while one was open for 9% of the time, Pallas kernels for 0%

commit v1 on v0

--- a/solution.py
+++ b/solution.py
@@ -6,6 +6,28 @@
 
 HEAD_DIM = 128
 CAP = 10
+
+
+def in_order(pieces, dim):
+    shape = list(pieces.shape[1:])
+    shape[dim] *= pieces.shape[0]
+    return jnp.moveaxis(pieces, 0, dim).reshape(shape)
+
+
+def gather_around(x, axis, dim):
+    size = lax.axis_size(axis)
+    pairs = [(i, (i + 1) % size) for i in range(size)]
+    back = [(b, a) for a, b in pairs]
+    lower, upper = ([], [])
+    for step in range(size - 1):
+        if step % 2 == 0:
+            lower.append(lax.ppermute(lower[-1] if lower else x, axis, pairs))
+        else:
+            upper.append(lax.ppermute(upper[-1] if upper else x, axis, back))
+    tiles = jnp.stack([*lower[::-1], x, *upper])
+    shift = lax.axis_index(axis) - len(lower)
+    tiles = tiles[(jnp.arange(size) - shift) % size]
+    return in_order(tiles, dim)
 
 
 def passed_along(value, axis, steps):
@@ -69,7 +91,7 @@
     )
     key_piece = lax.all_gather(key_rows[0], "blk", axis=0, tiled=True)
     value_fragment = lax.all_gather(value_rows[0], "blk", axis=0, tiled=True)
-    segment_piece = lax.all_gather(local_segment_labels, "blk", axis=0, tiled=True)
+    segment_piece = gather_around(local_segment_labels, "blk", 0)
     rows_in = key_piece.shape[0]
     width = math.gcd(rows_in, 512)
 

time: 132 us -> 135 us (1.023)
  blocking collectives: 43 us -> 32 us
  starting transfers between devices: 16.4 us -> 22.7 us
  waiting for transfers between devices: 30.4 us -> 35.6 us
    all_gather x1 -> x0, blocking collectives: 11.5 us -> none  [body(): lax.all_gather(local_segment_labels, 'blk', axis=0, tiled=True)]
    ppermute x0 -> x3, starting transfers between devices: none -> 6.65 us  [the longest x1 5.13 us: gather_around(): upper.append(lax.ppermute(upper[-1] if upper else x, axis, back))]
    all_to_all x1, waiting for transfers between devices: 0.01 us -> 4.62 us  [body(): lax.all_to_all(part_out, 'side', split_axis=1, concat_axis=1, tiled=True)]
    unnamed x13 -> x7, local copies, waits for them, and re-layouts: 3.93 us -> 4.66 us
  transfers between devices with their start and end apart: 5 -> 8, of which waited for: 3 -> 4; matrix products, arithmetic and copies ran while one was open for 9% -> 14% of each run, Pallas kernels for 0% -> 0%
where the time goes in v1:
time: 135 us; the launch traced here: 134 us
  waiting for transfers between devices  35.6 us (26%)
  blocking collectives  32 us (24%)
  starting transfers between devices  22.7 us (17%)
  between operations  14.2 us (11%)
  matrix products  12.8 us (9%)
  local copies, waits for them, and re-layouts  9.14 us (7%)
  other arithmetic  7.5 us (6%)
    ppermute x1, waiting for transfers between devices, passed_along(): return lax.ppermute(value, axis, pairs)  14.8 us
    psum x1, waiting for transfers between devices, body(): lax.psum(gate_part.astype(jnp.bfloat16), 'tp').astype(jnp.float32)  14.7 us
    all_gather x1, blocking collectives, body(): key_piece = lax.all_gather(key_rows[0], 'blk', axis=0, tiled=True)  14.1 us
    all_gather x1, blocking collectives, body(): value_fragment = lax.all_gather(value_rows[0], 'blk', axis=0, tiled=True)  12.3 us
    all_gather x1, blocking collectives, body(): shards = lax.all_gather(arrived, 'side', axis=1, tiled=True)  5.64 us
    ppermute x1, starting transfers between devices, gather_around(): upper.append(lax.ppermute(upper[-1] if upper else x, axis, back))  5.13 us
    all_to_all x1, starting transfers between devices, body(): lax.all_to_all(outgoing, 'blk', split_axis=0, concat_axis=0, tiled=True)  5.09 us
    all_to_all x1, starting transfers between devices, body(): lax.all_to_all(slot_out, 'blk', split_axis=0, concat_axis=0, tiled=True)  4.81 us
  transfers between devices with their start and end apart: 8, of which 4 were waited for; matrix products, arithmetic and copies ran while one was open for 14% of the time, Pallas kernels for 0%

profile of v1, /device:TPU:0, one launch (start us, length us, event | category | flops | bytes accessed | tf_op | source)
XLA Modules:
  0.0 134.1 jit_solution(9005777975512976800)
XLA Ops:
  7.2 5.1 %collective-permute-start.2 = (s32[128]{0:T(128)}, s32[128]{0:T(128)S(1)}, u32[]{:S(2)}, u32[]{:S(2)}) collective-permute-start(s32[128]{0:T(128)} %bitcast.139), channel_id=1, source_target_pairs={{4,0},{8,4},{12,8},{0,12},{5,1},{9,5},{13,9},{1,13},{6,2},{10,6},{... | collective-permute-start | bytes 1544 | tf_op jit(solution)/shard_map/ppermute | solution.py:26
  12.3 0.7 convert_reduce_fusion
  13.8 1.8 %gather_fusion.1 = bf16[20,2048]{1,0:T(8,128)(2,1)S(1)} fusion(bf16[128,2048]{1,0:T(8,128)(2,1)} %bitcast.129, s32[1024]{0:T(1024)S(1)} %pad_clamp_fusion), kind=kCustom, calls=%fused_computation.1 | custom fusion | bytes 163920 | tf_op jit(solution)/shard_map/jit(_take)/gather | solution.py:56
  15.6 0.7 fusion.47
  16.3 5.1 %all-to-all-start = ((bf16[4,1,10,1024]{3,2,1,0:T(8,128)(2,1)}), bf16[4,1,10,1024]{3,2,1,0:T(8,128)(2,1)S(1)}, u32[]{:S(2)}, u32[]{:S(2)}) async-start(bf16[4,1,10,1024]{3,2,1,0:T(8,128)(2,1)} %bitcast.25), calls=%async_computation | async-start | bytes 262144 | tf_op jit(solution)/shard_map/all_to_all | solution.py:150
  21.5 0.7 select_reduce_fusion.1
  22.2 14.1 %all-gather = bf16[1,512,128]{2,1,0:T(8,128)(2,1)S(1)} all-gather(bf16[1,128,128]{2,1,0:T(8,128)(2,1)} %param.11), channel_id=2, replica_groups=mesh['groups'=2,'blk'=4,'side'=2,'tp'=2] {'blk'}, dimensions={1}, use_global_device_ids=true | all-gather | bytes 163840 | tf_op jit(solution)/shard_map/all_gather | solution.py:92
  36.3 0.9 copy.45
  37.2 1.5 %collective-permute-start.1 = (s32[128]{0:T(128)S(1)}, s32[128]{0:T(128)S(1)}, u32[]{:S(2)}, u32[]{:S(2)}) collective-permute-start(s32[128]{0:T(128)S(1)} %collective-permute-done), channel_id=1, source_target_pairs={{0,4},{4,8},{8,12},{12,0},{1,5},{5,9},{9,13},{13,1},{2,6},{6,10},{... | collective-permute-start | bytes 1544 | tf_op jit(solution)/shard_map/ppermute | solution.py:24
  38.7 12.3 %all-gather.1 = bf16[1,512,128]{1,2,0:T(8,128)(2,1)S(1)} all-gather(bf16[1,128,128]{1,2,0:T(8,128)(2,1)S(1)} %copy.45), channel_id=3, replica_groups=mesh['groups'=2,'blk'=4,'side'=2,'tp'=2] {'blk'}, dimensions={1}, use_global_device_ids=true | all-gather | bytes 163840 | tf_op jit(solution)/shard_map/all_gather | solution.py:93
  51.0 1.1 copy.62
  52.1 0.7 pad_add_fusion
  53.4 0.8 fusion.41
  54.2 5.6 %all_gather.11 = bf16[4,2,10,1024]{3,2,1,0:T(8,128)(2,1)S(1)} all-gather(bf16[4,1,10,1024]{3,2,1,0:T(8,128)(2,1)S(1)} %all-to-all-done), channel_id=1, replica_groups=mesh['groups'=2,'blk'=4,'side'=2,'tp'=2] {'side'}, dimensions={1}, use_global_device_ids=true | all-gather | bytes 245760 | tf_op jit(solution)/shard_map/all_gather | solution.py:151
  59.8 2.5 %fusion.33 = bf16[1,4,2,10,768]{4,3,2,1,0:T(8,128)(2,1)} fusion(bf16[4,2,10,1024]{3,2,1,0:T(8,128)(2,1)S(1)} %all_gather.11, bf16[1,1024,768]{2,1,0:T(8,128)(2,1)} %param.17), kind=kOutput, calls=%fused_computation.25 | convolution fusion | flops 125890560 | bytes 1859584 | tf_op jit(solution)/shard_map/bscd,df->bscf/dot_general | solution.py:152
  62.3 2.5 %fusion.30 = bf16[1,4,2,10,768]{4,3,2,1,0:T(8,128)(2,1)} fusion(bf16[4,2,10,1024]{3,2,1,0:T(8,128)(2,1)S(1)} %all_gather.11, bf16[1,1024,768]{2,1,0:T(8,128)(2,1)} %param.18), kind=kOutput, calls=%fused_computation.24 | convolution fusion | flops 125890560 | bytes 1859584 | tf_op jit(solution)/shard_map/bscd,df->bscf/dot_general | solution.py:153
  64.8 2.7 %fusion = (f32[128,16]{0,1:T(8,128)S(1)}, f32[512,128,16]{1,0,2:T(8,128)}) fusion(pred[128,512]{0,1:T(8,128)(4,1)S(1)} %fusion.41, bf16[128,16,128]{2,1,0:T(8,128)(2,1)S(1)} %bitcast.128, bf16[1,512,128]{2,1,0:T(8,128)(2,1)S(1)} %all-gather), kind=kOutput, calls=%fused_computation.4 | convolution fusion | flops 271579136 | bytes 4923392 | tf_op jit(solution)/shard_map/while/body/eval_jaxpr/wsmz,usz->wsmu/dot_general | solution.py:114
  67.5 14.7 %all-reduce.3.cloned.1.call-done = (bf16[1,4,2,10,768]{4,3,2,1,0:T(8,128)(2,1)}, bf16[1,4,2,10,768]{4,3,2,1,0:T(8,128)(2,1)}) async-done(((bf16[1,4,2,10,768]{4,3,2,1,0:T(8,128)(2,1)}, bf16[1,4,2,10,768]{4,3,2,1,0:T(8,128)(2,1)}), (bf16[1,4,2,10,768]{4,3,2,1,0:T(8,128)(2,1)}, bf16[1,4,2,10,768]{4,3,2,1,0:T(8,128)(2,1)})) %all-reduce.3.cloned.1.call-update) | async-done | bytes 245776 | tf_op jit(solution)/shard_map/psum | solution.py:158
  82.1 0.9 constant_dynamic-update-slice_fusion.1
  83.1 0.9 constant_dynamic-update-slice_fusion
  84.0 2.8 %collective-permute-start.3 = (bf16[2,4,2,10,768]{4,3,2,1,0:T(8,128)(2,1)S(1)}, bf16[2,4,2,10,768]{4,3,2,1,0:T(8,128)(2,1)S(1)}, u32[]{:S(2)}, u32[]{:S(2)}) collective-permute-start(bf16[2,4,2,10,768]{4,3,2,1,0:T(8,128)(2,1)S(1)} %constant_dynamic-update-slice_fusion), channel_id=1, source_target_pairs={{0,8},{4,12},{8,0},{12,4},{1,9},{5,13},{9,1},{13,5},{2,10},{6,14},... | collective-permute-start | bytes 737288 | tf_op jit(solution)/shard_map/ppermute | solution.py:36
  86.8 3.2 %fusion.1 = f32[128,16]{0,1:T(8,128)S(1)} fusion(f32[512,128,16]{1,0,2:T(8,128)} %get-tuple-element.48, f32[128,16]{0,1:T(8,128)S(1)} %broadcast_maximum_fusion, pred[128,512]{0,1:T(8,128)(4,1)S(1)} %fusion.41), kind=kLoop, calls=%fused_computation.5 | loop fusion | flops 5240832 | bytes 4276224 | tf_op jit(solution)/shard_map/while/body/eval_jaxpr/reduce_sum | solution.py:123
  90.0 14.8 %collective-permute-done.3 = bf16[2,4,2,10,768]{4,3,2,1,0:T(8,128)(2,1)S(1)} collective-permute-done((bf16[2,4,2,10,768]{4,3,2,1,0:T(8,128)(2,1)S(1)}, bf16[2,4,2,10,768]{4,3,2,1,0:T(8,128)(2,1)S(1)}, u32[]{:S(2)}, u32[]{:S(2)}) %collective-permute-start.3) | collective-permute-done | bytes 245792 | tf_op jit(solution)/shard_map/ppermute | solution.py:36
  105.3 0.8 copy.51
  106.1 3.4 %all-to-all-start.1 = ((bf16[4,2,10,1024]{3,0,2,1:T(4,128)(2,1)}), bf16[4,2,10,1024]{3,0,2,1:T(4,128)(2,1)S(1)}, u32[]{:S(2)}, u32[]{:S(2)}) async-start(bf16[4,2,10,1024]{3,0,2,1:T(4,128)(2,1)} %copy.51), calls=%async_computation.1 | async-start | bytes 327680 | tf_op jit(solution)/shard_map/all_to_all | solution.py:170
  109.6 4.6 %all-to-all-done.1 = bf16[4,2,10,1024]{3,0,2,1:T(4,128)(2,1)S(1)} async-done(((bf16[4,2,10,1024]{3,0,2,1:T(4,128)(2,1)}), bf16[4,2,10,1024]{3,0,2,1:T(4,128)(2,1)S(1)}, u32[]{:S(2)}, u32[]{:S(2)}) %all-to-all-start.1) | async-done | bytes 163872 | tf_op jit(solution)/shard_map/all_to_all | solution.py:170
  114.3 0.7 copy.61
  115.0 4.8 %all-to-all-start.2 = ((bf16[4,10,1024]{2,1,0:T(8,128)(2,1)}), bf16[4,10,1024]{2,1,0:T(8,128)(2,1)S(1)}, u32[]{:S(2)}, u32[]{:S(2)}) async-start(bf16[4,10,1024]{2,1,0:T(8,128)(2,1)} %copy.61), calls=%async_computation.2 | async-start | bytes 262144 | tf_op jit(solution)/shard_map/all_to_all | solution.py:172
  119.8 3.4 %divide_convert_fusion = bf16[1,128,128,16]{2,1,3,0:T(8,128)(2,1)S(1)} fusion(f32[512,128,16]{1,0,2:T(8,128)} %get-tuple-element.48, f32[128,16]{0,1:T(8,128)S(1)} %broadcast_maximum_fusion, pred[128,512]{0,1:T(8,128)(4,1)S(1)} %fusion.41, f32[128,16]{0,1:T(8,128)S(1)} %get-tuple-element.46, f32[128,16]{0,1:T(8,128)S(1)} %get-tuple-element.45, ...), kind=kOutput, calls=%fused_computation.26 | convolution fusion | flops 274464768 | bytes 4939776 | tf_op jit(solution)/shard_map/while/body/eval_jaxpr/jzre,ezm->jzrm/dot_general | solution.py:124
  123.2 1.0 copy.55
  124.2 1.5 %all-to-all-done.2 = bf16[4,10,1024]{2,1,0:T(8,128)(2,1)S(1)} async-done(((bf16[4,10,1024]{2,1,0:T(8,128)(2,1)}), bf16[4,10,1024]{2,1,0:T(8,128)(2,1)S(1)}, u32[]{:S(2)}, u32[]{:S(2)}) %all-to-all-start.2) | async-done | bytes 81952 | tf_op jit(solution)/shard_map/all_to_all | solution.py:172
  125.8 1.4 %fusion.4 = bf16[1,128,2048]{2,1,0:T(8,128)(2,1)} fusion(bf16[2048,10,2]{0,2,1:T(2,128)(2,1)S(1)} %bitcast.130, f32[2,128]{1,0:T(2,128)S(1)} %bitcast.137, s32[2,128]{1,0:T(2,128)S(1)} %copy.49, pred[2,128]{1,0:T(4,128)(4,1)S(1)} %compare_bitcast_fusion), kind=kOutput, calls=%fused_computation.9 | convolution fusion | flops 63184384 | bytes 608512 | tf_op jit(solution)/shard_map/ecr,kecq->rkq/dot_general | solution.py:175
  (31 shorter events, 2.1 us)
Async XLA Ops:
  7.2 97.7 %copy-start = (bf16[1,768,1024]{2,1,0:T(8,128)(2,1)S(1)}, bf16[1,768,1024]{2,1,0:T(8,128)(2,1)}, u32[]{:S(2)}) copy-start(bf16[1,768,1024]{2,1,0:T(8,128)(2,1)} %param.19) | copy-start | bytes 4718596
  7.2 45.0 %collective-permute-start.2 = (s32[128]{0:T(128)}, s32[128]{0:T(128)S(1)}, u32[]{:S(2)}, u32[]{:S(2)}) collective-permute-start(s32[128]{0:T(128)} %bitcast.139), channel_id=1, source_target_pairs={{4,0},{8,4},{12,8},{0,12},{5,1},{9,5},{13,9},{1,13},{6,2},{10,6},{... | collective-permute-start | bytes 1544 | tf_op jit(solution)/shard_map/ppermute | solution.py:26
  12.3 24.9 %collective-permute-start = (s32[128]{0:T(128)}, s32[128]{0:T(128)S(1)}, u32[]{:S(2)}, u32[]{:S(2)}) collective-permute-start(s32[128]{0:T(128)} %bitcast.140), channel_id=1, source_target_pairs={{0,4},{4,8},{8,12},{12,0},{1,5},{5,9},{9,13},{13,1},{2,6},{6,10},{... | collective-permute-start | bytes 1544 | tf_op jit(solution)/shard_map/ppermute | solution.py:24
  16.3 37.8 %all-to-all-start = ((bf16[4,1,10,1024]{3,2,1,0:T(8,128)(2,1)}), bf16[4,1,10,1024]{3,2,1,0:T(8,128)(2,1)S(1)}, u32[]{:S(2)}, u32[]{:S(2)}) async-start(bf16[4,1,10,1024]{3,2,1,0:T(8,128)(2,1)} %bitcast.25), calls=%async_computation | async-start | bytes 262144 | tf_op jit(solution)/shard_map/all_to_all | solution.py:150
  21.4 60.7 %all-reduce.3.cloned.1.call-start = ((), (), s32[]{:S(2)}) async-start(), calls=%async_computation.3 | async-start | bytes 786432 | tf_op jit(solution)/shard_map/psum | solution.py:158
  37.2 15.0 %collective-permute-start.1 = (s32[128]{0:T(128)S(1)}, s32[128]{0:T(128)S(1)}, u32[]{:S(2)}, u32[]{:S(2)}) collective-permute-start(s32[128]{0:T(128)S(1)} %collective-permute-done), channel_id=1, source_target_pairs={{0,4},{4,8},{8,12},{12,0},{1,5},{5,9},{9,13},{13,1},{2,6},{6,10},{... | collective-permute-start | bytes 1544 | tf_op jit(solution)/shard_map/ppermute | solution.py:24
  84.0 20.7 %collective-permute-start.3 = (bf16[2,4,2,10,768]{4,3,2,1,0:T(8,128)(2,1)S(1)}, bf16[2,4,2,10,768]{4,3,2,1,0:T(8,128)(2,1)S(1)}, u32[]{:S(2)}, u32[]{:S(2)}) collective-permute-start(bf16[2,4,2,10,768]{4,3,2,1,0:T(8,128)(2,1)S(1)} %constant_dynamic-update-slice_fusion), channel_id=1, source_target_pairs={{0,8},{4,12},{8,0},{12,4},{1,9},{5,13},{9,1},{13,5},{2,10},{6,14},... | collective-permute-start | bytes 737288 | tf_op jit(solution)/shard_map/ppermute | solution.py:36
  106.1 8.1 %all-to-all-start.1 = ((bf16[4,2,10,1024]{3,0,2,1:T(4,128)(2,1)}), bf16[4,2,10,1024]{3,0,2,1:T(4,128)(2,1)S(1)}, u32[]{:S(2)}, u32[]{:S(2)}) async-start(bf16[4,2,10,1024]{3,0,2,1:T(4,128)(2,1)} %copy.51), calls=%async_computation.1 | async-start | bytes 327680 | tf_op jit(solution)/shard_map/all_to_all | solution.py:170
  115.0 10.7 %all-to-all-start.2 = ((bf16[4,10,1024]{2,1,0:T(8,128)(2,1)}), bf16[4,10,1024]{2,1,0:T(8,128)(2,1)S(1)}, u32[]{:S(2)}, u32[]{:S(2)}) async-start(bf16[4,10,1024]{2,1,0:T(8,128)(2,1)} %copy.61), calls=%async_computation.2 | async-start | bytes 262144 | tf_op jit(solution)/shard_map/all_to_all | solution.py:172
Sparse Core Ops, SparseCore 0:
  64.9 17.2 all-reduce.2
